TPU v7x, 256 devices: a whole 4x4x8 slice. The times are simulated.
256 devices in a mesh: tile: 64 (over z, y_lo, x), chan: 4 (over y_hi, core).
Axes of the slice: x: 4, y: 4 (y_hi: 2, y_lo: 2; y = y_hi * 2 + y_lo), z: 8, core: 2. Of those that a mesh axis runs over, the one named last changes fastest.
Arguments:
- latent: bfloat16 [2, 16, 14400], P(None, 'chan', 'tile'), may hold values from -6 to 6
- latent_cache: bfloat16 [2, 16, 14400], P(None, 'chan', 'tile'), may hold values from -6 to 6
- weight_in: bfloat16 [3, 3, 3, 384, 16], P(None, None, None, 'chan'), may hold values from -0.3125 to 0.3125
- bias_in: float32 [384], P('chan'), may hold values from -3 to 3
- cache_a: bfloat16 [2, 384, 14400], P(None, 'chan', 'tile'), may hold values from -6 to 6
- gain_a: float32 [384], P('chan'), may hold values from 0.1 to 1.9
- weight_a: bfloat16 [3, 3, 3, 384, 384], P(None, None, None, 'chan'), may hold values from -0.0625 to 0.0625
- bias_a: float32 [384], P('chan'), may hold values from -3 to 3
- cache_b: bfloat16 [2, 384, 14400], P(None, 'chan', 'tile'), may hold values from -6 to 6
- gain_b: float32 [384], P('chan'), may hold values from 0.1 to 1.9
- weight_b: bfloat16 [3, 3, 3, 384, 384], P(None, None, None, 'chan'), may hold values from -0.0625 to 0.0625
- bias_b: float32 [384], P('chan'), may hold values from -3 to 3
- weight_up: bfloat16 [3, 3, 192, 384], P(None, None, 'chan'), may hold values from -0.109375 to 0.109375
- bias_up: float32 [192], P('chan'), may hold values from -3 to 3
Outputs:
- upsampled: bfloat16 [2, 192, 57600], P(None, 'chan', 'tile')
All inputs are finite; a program needn't handle non-finite values.
Results may differ from a plain program's by a relative error of at most 0.011.
Values may be sent and summed in bfloat16 or wider, within the bound.
A program may use at most 64 MiB of HBM per device.

v0:
```python
from functools import partial

import jax
import jax.numpy as jnp
from jax import lax
from jax.sharding import PartitionSpec as P

C = 384
W = 160


eps_norm = 1e-06


def extended(block, sides, width):
    for axis, dim in sides:
        count = lax.axis_size(axis)
        forward = [(i, i + 1) for i in range(count - 1)]
        backward = [(target, source) for source, target in forward]
        low = lax.ppermute(
            lax.slice_in_dim(block, block.shape[dim] - width, None, axis=dim), axis, forward
        )
        high = lax.ppermute(lax.slice_in_dim(block, 0, width, axis=dim), axis, backward)
        block = jnp.concatenate([low, block, high], axis=dim)
    return block


def column_mask(part, column_tap, position):
    if column_tap == 0:
        return jnp.where(position > 0, part, 0.0)
    if column_tap == 2:
        return jnp.where(position < W - 1, part, 0.0)
    return part


def causal_terms(source, weight_rows, start):
    frames = source.shape[0] - 2
    count = source.shape[2] - 2 * W - 2
    position = (start + lax.iota(jnp.int32, count)) % W
    outputs = weight_rows.shape[3]
    summed = jnp.zeros((frames, outputs, count), jnp.float32)
    for column_tap in range(3):
        part = jnp.zeros((frames, outputs, count), jnp.float32)
        for time_tap in range(3):
            for row_tap in range(3):
                begin = row_tap * W + column_tap
                window = source[time_tap : time_tap + frames, :, begin : begin + count]
                part = part + jnp.einsum(
                    "ok,fkr->for",
                    weight_rows[time_tap, row_tap, column_tap],
                    window,
                    preferred_element_type=jnp.float32,
                )
        summed = summed + column_mask(part, column_tap, position)
    return summed


def upsample_terms(source, weight_rows, start):
    frames = source.shape[0]
    count = source.shape[2] - 2 * W - 2
    position = (start + lax.iota(jnp.int32, count)) % W
    outputs = weight_rows.shape[2]
    quarters = []
    for row_half in range(2):
        for column_half in range(2):
            summed = jnp.zeros((frames, outputs, count), jnp.float32)
            for column_step in range(3):
                part = jnp.zeros((frames, outputs, count), jnp.float32)
                for row_tap in range(3):
                    row_step = (row_half + row_tap - 1) // 2
                    for column_tap in range(3):
                        if (column_half + column_tap - 1) // 2 != column_step - 1:
                            continue
                        begin = (row_step + 1) * W + column_step
                        window = source[:, :, begin : begin + count]
                        part = part + jnp.einsum(
                            "ok,fkr->for",
                            weight_rows[row_tap, column_tap],
                            window,
                            preferred_element_type=jnp.float32,
                        )
                summed = summed + column_mask(part, column_step, position)
            quarters.append(summed)
    stacked = jnp.stack(quarters, -1)
    return stacked.reshape(frames, outputs, 4 * count)


def convolve(source, weight, kernel_fn):
    complete = lax.all_gather(source, "chan", axis=1, tiled=True)
    rimmed = extended(complete, (("tile", 2),), W + 1)
    return kernel_fn(rimmed, weight)


def activate(features, gain_vector):
    values = features.astype(jnp.float32)
    squares = jnp.sum(values * values, axis=1)
    total_sq = lax.psum(squares, "chan")
    inverse_rms = lax.rsqrt(total_sq / C + eps_norm)
    return jax.nn.silu(values * inverse_rms[:, None, :] * gain_vector[None, :, None]).astype(
        jnp.bfloat16
    )


def shards(
    latent,
    latent_cache,
    weight_in,
    bias_in,
    cache_a,
    gain_a,
    weight_a,
    bias_a,
    cache_b,
    gain_b,
    weight_b,
    bias_b,
    weight_up,
    bias_up,
):
    span = latent.shape[2]
    start = lax.axis_index("tile") * span
    causal_fn = partial(causal_terms, start=start)
    upsample_fn = partial(upsample_terms, start=start)
    stem_sum = convolve(jnp.concatenate([latent_cache, latent], 0), weight_in, causal_fn)
    stem_out = (stem_sum + bias_in[None, :, None]).astype(jnp.bfloat16)
    active_a = activate(stem_out, gain_a)
    inner_sum = convolve(jnp.concatenate([cache_a, active_a], 0), weight_a, causal_fn)
    inner_out = (inner_sum + bias_a[None, :, None]).astype(jnp.bfloat16)
    active_b = activate(inner_out, gain_b)
    branch_sum = convolve(jnp.concatenate([cache_b, active_b], 0), weight_b, causal_fn)
    residual_out = (stem_out.astype(jnp.float32) + branch_sum + bias_b[None, :, None]).astype(
        jnp.bfloat16
    )
    upsample_sum = convolve(residual_out, weight_up, upsample_fn)
    return (upsample_sum + bias_up[None, :, None]).astype(jnp.bfloat16)


def solution(mesh):
    placed = (
        P(None, "chan", "tile"),
        P(None, "chan", "tile"),
        P(None, None, None, "chan", None),
        P("chan"),
        P(None, "chan", "tile"),
        P("chan"),
        P(None, None, None, "chan", None),
        P("chan"),
        P(None, "chan", "tile"),
        P("chan"),
        P(None, None, None, "chan", None),
        P("chan"),
        P(None, None, "chan", None),
        P("chan"),
    )
    return jax.shard_map(
        shards, mesh=mesh, in_specs=placed, out_specs=P(None, "chan", "tile"), check_vma=False
    )
```

profile of v0, /device:TPU:128, one launch (start us, length us, event | category | flops | bytes accessed | tf_op | source)
XLA Modules:
  0.0 182.4 jit_solution(865237823081435494)
XLA Ops:
  1.4 6.7 %all_gather.12 = bf16[4,16,225]{2,0,1:T(4,128)(2,1)S(1)} all-gather(bf16[4,4,225]{2,0,1:T(4,128)(2,1)S(1)} %pad_maximum_fusion.19), channel_id=1, replica_groups=mesh['tile'=64,'chan'=4] {'chan'}, dimensions={1}, use_global_device_ids=true | all-gather | bytes 36000 | tf_op jit(solution)/shard_map/all_gather | solution.py:89
  8.2 5.2 %collective-permute-start.1 = (bf16[4,16,161]{2,1,0:T(8,128)(2,1)S(1)}, bf16[4,16,161]{2,1,0:T(8,128)(2,1)S(1)}, u32[]{:S(2)}, u32[]{:S(2)}) collective-permute-start(bf16[4,16,161]{2,1,0:T(8,128)(2,1)S(1)} %get-tuple-element.18), channel_id=1, source_target_pairs={{4,0},{8,4},{12,8},{16,12},{20,16},{24,20},{28,24},{32,28},{36,32}... | collective-permute-start | bytes 61832 | tf_op jit(solution)/shard_map/ppermute | solution.py:23
  13.4 1.9 %collective-permute-start = (bf16[4,16,161]{2,1,0:T(8,128)(2,1)S(1)}, bf16[4,16,161]{2,1,0:T(8,128)(2,1)S(1)}, u32[]{:S(2)}, u32[]{:S(2)}) collective-permute-start(bf16[4,16,161]{2,1,0:T(8,128)(2,1)S(1)} %get-tuple-element.17), channel_id=1, source_target_pairs={{0,4},{4,8},{8,12},{12,16},{16,20},{20,24},{24,28},{28,32},{32,36}... | collective-permute-start | bytes 61832 | tf_op jit(solution)/shard_map/ppermute | solution.py:20
  28.5 8.6 %psum.14 = f32[2,225]{1,0:T(2,128)S(1)} all-reduce(f32[2,225]{1,0:T(2,128)S(1)} %get-tuple-element.19), channel_id=1, replica_groups=mesh['tile'=64,'chan'=4] {'chan'}, use_global_device_ids=true, to_apply=%region_1.2 | all-reduce | flops 450 | bytes 3600 | tf_op jit(solution)/shard_map/psum | solution.py:97
  37.3 8.9 %all_gather.13 = bf16[4,384,225]{2,1,0:T(8,128)(2,1)S(1)} all-gather(bf16[4,96,225]{2,1,0:T(8,128)(2,1)S(1)} %pad_maximum_fusion.13), channel_id=1, replica_groups=mesh['tile'=64,'chan'=4] {'chan'}, dimensions={1}, use_global_device_ids=true | all-gather | bytes 864000 | tf_op jit(solution)/shard_map/all_gather | solution.py:89
  47.4 6.6 %collective-permute-start.3 = (bf16[4,384,161]{1,0,2:T(4,128)(2,1)S(1)}, bf16[4,384,161]{1,0,2:T(4,128)(2,1)}, u32[]{:S(2)}, u32[]{:S(2)}) collective-permute-start(bf16[4,384,161]{1,0,2:T(4,128)(2,1)S(1)} %copy.259), channel_id=1, source_target_pairs={{4,0},{8,4},{12,8},{16,12},{20,16},{24,20},{28,24},{32,28},{36,32}... | collective-permute-start | bytes 1483784 | tf_op jit(solution)/shard_map/ppermute | solution.py:23
  54.9 1.9 %collective-permute-start.2 = (bf16[4,384,161]{1,0,2:T(4,128)(2,1)S(1)}, bf16[4,384,161]{1,0,2:T(4,128)(2,1)}, u32[]{:S(2)}, u32[]{:S(2)}) collective-permute-start(bf16[4,384,161]{1,0,2:T(4,128)(2,1)S(1)} %copy.255), channel_id=1, source_target_pairs={{0,4},{4,8},{8,12},{12,16},{16,20},{20,24},{24,28},{28,32},{32,36}... | collective-permute-start | bytes 1483784 | tf_op jit(solution)/shard_map/ppermute | solution.py:20
  57.9 1.8 fusion.301
  59.7 1.8 fusion.305
  61.5 3.6 %collective-permute-done.3 = bf16[4,384,161]{1,0,2:T(4,128)(2,1)} collective-permute-done((bf16[4,384,161]{1,0,2:T(4,128)(2,1)S(1)}, bf16[4,384,161]{1,0,2:T(4,128)(2,1)}, u32[]{:S(2)}, u32[]{:S(2)}) %collective-permute-start.3) | collective-permute-done | bytes 494624 | tf_op jit(solution)/shard_map/ppermute | solution.py:23
  71.7 2.6 %collective-permute-done.2 = bf16[4,384,161]{1,0,2:T(4,128)(2,1)} collective-permute-done((bf16[4,384,161]{1,0,2:T(4,128)(2,1)S(1)}, bf16[4,384,161]{1,0,2:T(4,128)(2,1)}, u32[]{:S(2)}, u32[]{:S(2)}) %collective-permute-start.2) | collective-permute-done | bytes 494624 | tf_op jit(solution)/shard_map/ppermute | solution.py:20
  86.1 8.7 %psum.15 = f32[2,225]{1,0:T(2,128)S(1)} all-reduce(f32[2,225]{1,0:T(2,128)S(1)} %get-tuple-element.21), channel_id=1, replica_groups=mesh['tile'=64,'chan'=4] {'chan'}, use_global_device_ids=true, to_apply=%region_3.4 | all-reduce | flops 450 | bytes 3600 | tf_op jit(solution)/shard_map/psum | solution.py:97
  95.0 8.7 %all_gather.14 = bf16[4,384,225]{2,1,0:T(8,128)(2,1)S(1)} all-gather(bf16[4,96,225]{2,1,0:T(8,128)(2,1)S(1)} %pad_maximum_fusion.14), channel_id=1, replica_groups=mesh['tile'=64,'chan'=4] {'chan'}, dimensions={1}, use_global_device_ids=true | all-gather | bytes 864000 | tf_op jit(solution)/shard_map/all_gather | solution.py:89
  104.9 5.8 %collective-permute-start.5 = (bf16[4,384,161]{1,0,2:T(4,128)(2,1)S(1)}, bf16[4,384,161]{1,0,2:T(4,128)(2,1)}, u32[]{:S(2)}, u32[]{:S(2)}) collective-permute-start(bf16[4,384,161]{1,0,2:T(4,128)(2,1)S(1)} %copy.290), channel_id=1, source_target_pairs={{4,0},{8,4},{12,8},{16,12},{20,16},{24,20},{28,24},{32,28},{36,32}... | collective-permute-start | bytes 1483784 | tf_op jit(solution)/shard_map/ppermute | solution.py:23
  111.6 1.9 %collective-permute-start.4 = (bf16[4,384,161]{1,0,2:T(4,128)(2,1)S(1)}, bf16[4,384,161]{1,0,2:T(4,128)(2,1)}, u32[]{:S(2)}, u32[]{:S(2)}) collective-permute-start(bf16[4,384,161]{1,0,2:T(4,128)(2,1)S(1)} %copy.286), channel_id=1, source_target_pairs={{0,4},{4,8},{8,12},{12,16},{16,20},{20,24},{24,28},{28,32},{32,36}... | collective-permute-start | bytes 1483784 | tf_op jit(solution)/shard_map/ppermute | solution.py:20
  114.7 1.8 fusion.271
  116.4 1.8 fusion.275
  118.2 3.6 %collective-permute-done.5 = bf16[4,384,161]{1,0,2:T(4,128)(2,1)} collective-permute-done((bf16[4,384,161]{1,0,2:T(4,128)(2,1)S(1)}, bf16[4,384,161]{1,0,2:T(4,128)(2,1)}, u32[]{:S(2)}, u32[]{:S(2)}) %collective-permute-start.5) | collective-permute-done | bytes 494624 | tf_op jit(solution)/shard_map/ppermute | solution.py:23
  128.5 2.6 %collective-permute-done.4 = bf16[4,384,161]{1,0,2:T(4,128)(2,1)} collective-permute-done((bf16[4,384,161]{1,0,2:T(4,128)(2,1)S(1)}, bf16[4,384,161]{1,0,2:T(4,128)(2,1)}, u32[]{:S(2)}, u32[]{:S(2)}) %collective-permute-start.4) | collective-permute-done | bytes 494624 | tf_op jit(solution)/shard_map/ppermute | solution.py:20
  142.9 7.7 %all_gather.15 = bf16[2,384,225]{2,1,0:T(8,128)(2,1)S(1)} all-gather(bf16[2,96,225]{2,1,0:T(8,128)(2,1)S(1)} %fusion.76), channel_id=1, replica_groups=mesh['tile'=64,'chan'=4] {'chan'}, dimensions={1}, use_global_device_ids=true | all-gather | bytes 432000 | tf_op jit(solution)/shard_map/all_gather | solution.py:89
  151.5 6.1 %collective-permute-start.7 = (bf16[2,384,161]{2,1,0:T(8,128)(2,1)S(1)}, bf16[2,384,161]{2,1,0:T(8,128)(2,1)S(1)}, u32[]{:S(2)}, u32[]{:S(2)}) collective-permute-start(bf16[2,384,161]{2,1,0:T(8,128)(2,1)S(1)} %get-tuple-element.16), channel_id=1, source_target_pairs={{4,0},{8,4},{12,8},{16,12},{20,16},{24,20},{28,24},{32,28},{36,32}... | collective-permute-start | bytes 741896 | tf_op jit(solution)/shard_map/ppermute | solution.py:23
  157.6 2.1 %collective-permute-start.6 = (bf16[2,384,161]{2,1,0:T(8,128)(2,1)S(1)}, bf16[2,384,161]{2,1,0:T(8,128)(2,1)S(1)}, u32[]{:S(2)}, u32[]{:S(2)}) collective-permute-start(bf16[2,384,161]{2,1,0:T(8,128)(2,1)S(1)} %get-tuple-element.15), channel_id=1, source_target_pairs={{0,4},{4,8},{8,12},{12,16},{16,20},{20,24},{24,28},{28,32},{32,36}... | collective-permute-start | bytes 741896 | tf_op jit(solution)/shard_map/ppermute | solution.py:20
  160.1 6.3 %collective-permute-done.7 = bf16[2,384,161]{2,1,0:T(8,128)(2,1)S(1)} collective-permute-done((bf16[2,384,161]{2,1,0:T(8,128)(2,1)S(1)}, bf16[2,384,161]{2,1,0:T(8,128)(2,1)S(1)}, u32[]{:S(2)}, u32[]{:S(2)}) %collective-permute-start.7) | collective-permute-done | bytes 247328 | tf_op jit(solution)/shard_map/ppermute | solution.py:23
  166.5 8.3 %collective-permute-done.6 = bf16[2,384,161]{2,1,0:T(8,128)(2,1)S(1)} collective-permute-done((bf16[2,384,161]{2,1,0:T(8,128)(2,1)S(1)}, bf16[2,384,161]{2,1,0:T(8,128)(2,1)S(1)}, u32[]{:S(2)}, u32[]{:S(2)}) %collective-permute-start.6) | collective-permute-done | bytes 247328 | tf_op jit(solution)/shard_map/ppermute | solution.py:20
  (164 shorter events, 66.3 us)
Async XLA Ops:
  0.0 23.5 %copy-start.7 = (bf16[3,3,3,96,16]{3,4,2,1,0:T(8,128)(2,1)S(1)}, bf16[3,3,3,96,16]{3,4,2,1,0:T(8,128)(2,1)}, u32[]{:S(2)}) copy-start(bf16[3,3,3,96,16]{3,4,2,1,0:T(8,128)(2,1)} %param.16) | copy-start | bytes 248836
  8.2 9.9 %collective-permute-start.1 = (bf16[4,16,161]{2,1,0:T(8,128)(2,1)S(1)}, bf16[4,16,161]{2,1,0:T(8,128)(2,1)S(1)}, u32[]{:S(2)}, u32[]{:S(2)}) collective-permute-start(bf16[4,16,161]{2,1,0:T(8,128)(2,1)S(1)} %get-tuple-element.18), channel_id=1, source_target_pairs={{4,0},{8,4},{12,8},{16,12},{20,16},{24,20},{28,24},{32,28},{36,32}... | collective-permute-start | bytes 61832 | tf_op jit(solution)/shard_map/ppermute | solution.py:23
  13.4 10.0 %collective-permute-start = (bf16[4,16,161]{2,1,0:T(8,128)(2,1)S(1)}, bf16[4,16,161]{2,1,0:T(8,128)(2,1)S(1)}, u32[]{:S(2)}, u32[]{:S(2)}) collective-permute-start(bf16[4,16,161]{2,1,0:T(8,128)(2,1)S(1)} %get-tuple-element.17), channel_id=1, source_target_pairs={{0,4},{4,8},{8,12},{12,16},{16,20},{20,24},{24,28},{28,32},{32,36}... | collective-permute-start | bytes 61832 | tf_op jit(solution)/shard_map/ppermute | solution.py:20
  27.6 0.7 copy-start.10
  27.6 9.5 %copy-start.11 = (f32[96]{0:T(128)S(1)}, f32[96]{0:T(128)}, u32[]{:S(2)}) copy-start(f32[96]{0:T(128)} %param.19) | copy-start | bytes 1156
  27.6 9.6 %copy-start.8 = (bf16[2,96,225]{2,1,0:T(8,128)(2,1)S(1)}, bf16[2,96,225]{2,1,0:T(8,128)(2,1)}, u32[]{:S(2)}) copy-start(bf16[2,96,225]{2,1,0:T(8,128)(2,1)} %param.18) | copy-start | bytes 259204
  47.4 17.6 %collective-permute-start.3 = (bf16[4,384,161]{1,0,2:T(4,128)(2,1)S(1)}, bf16[4,384,161]{1,0,2:T(4,128)(2,1)}, u32[]{:S(2)}, u32[]{:S(2)}) collective-permute-start(bf16[4,384,161]{1,0,2:T(4,128)(2,1)S(1)} %copy.259), channel_id=1, source_target_pairs={{4,0},{8,4},{12,8},{16,12},{20,16},{24,20},{28,24},{32,28},{36,32}... | collective-permute-start | bytes 1483784 | tf_op jit(solution)/shard_map/ppermute | solution.py:23
  54.9 19.5 %collective-permute-start.2 = (bf16[4,384,161]{1,0,2:T(4,128)(2,1)S(1)}, bf16[4,384,161]{1,0,2:T(4,128)(2,1)}, u32[]{:S(2)}, u32[]{:S(2)}) collective-permute-start(bf16[4,384,161]{1,0,2:T(4,128)(2,1)S(1)} %copy.255), channel_id=1, source_target_pairs={{0,4},{4,8},{8,12},{12,16},{16,20},{20,24},{24,28},{28,32},{32,36}... | collective-permute-start | bytes 1483784 | tf_op jit(solution)/shard_map/ppermute | solution.py:20
  75.9 2.7 %copy-start.1 = (bf16[3,3,3,96,384]{4,3,2,1,0:T(8,128)(2,1)S(1)}, bf16[3,3,3,96,384]{4,3,2,1,0:T(8,128)(2,1)}, u32[]{:S(2)}) copy-start(bf16[3,3,3,96,384]{4,3,2,1,0:T(8,128)(2,1)} %param.20) | copy-start | bytes 5971972
  82.7 0.9 copy-start.3
  82.7 1.0 copy-start.4
  85.0 0.7 copy-start.12
  85.7 9.1 %copy-start.13 = (f32[96]{0:T(128)S(1)}, f32[96]{0:T(128)}, u32[]{:S(2)}) copy-start(f32[96]{0:T(128)} %param.23) | copy-start | bytes 1156
  85.7 9.3 %copy-start.9 = (bf16[2,96,225]{2,1,0:T(8,128)(2,1)S(1)}, bf16[2,96,225]{2,1,0:T(8,128)(2,1)}, u32[]{:S(2)}) copy-start(bf16[2,96,225]{2,1,0:T(8,128)(2,1)} %param.22) | copy-start | bytes 259204
  104.9 16.9 %collective-permute-start.5 = (bf16[4,384,161]{1,0,2:T(4,128)(2,1)S(1)}, bf16[4,384,161]{1,0,2:T(4,128)(2,1)}, u32[]{:S(2)}, u32[]{:S(2)}) collective-permute-start(bf16[4,384,161]{1,0,2:T(4,128)(2,1)S(1)} %copy.290), channel_id=1, source_target_pairs={{4,0},{8,4},{12,8},{16,12},{20,16},{24,20},{28,24},{32,28},{36,32}... | collective-permute-start | bytes 1483784 | tf_op jit(solution)/shard_map/ppermute | solution.py:23
  111.6 19.5 %collective-permute-start.4 = (bf16[4,384,161]{1,0,2:T(4,128)(2,1)S(1)}, bf16[4,384,161]{1,0,2:T(4,128)(2,1)}, u32[]{:S(2)}, u32[]{:S(2)}) collective-permute-start(bf16[4,384,161]{1,0,2:T(4,128)(2,1)S(1)} %copy.286), channel_id=1, source_target_pairs={{0,4},{4,8},{8,12},{12,16},{16,20},{20,24},{24,28},{28,32},{32,36}... | collective-permute-start | bytes 1483784 | tf_op jit(solution)/shard_map/ppermute | solution.py:20
  132.7 2.7 %copy-start.2 = (bf16[3,3,3,96,384]{4,3,2,1,0:T(8,128)(2,1)S(1)}, bf16[3,3,3,96,384]{4,3,2,1,0:T(8,128)(2,1)}, u32[]{:S(2)}) copy-start(bf16[3,3,3,96,384]{4,3,2,1,0:T(8,128)(2,1)} %param.24) | copy-start | bytes 5971972
  139.5 0.9 copy-start.5
  139.5 1.0 copy-start.6
  141.8 0.7 copy-start.15
  142.4 8.3 %copy-start = (bf16[3,3,48,384]{3,2,1,0:T(8,128)(2,1)S(1)}, bf16[3,3,48,384]{3,2,1,0:T(8,128)(2,1)}, u32[]{:S(2)}) copy-start(bf16[3,3,48,384]{3,2,1,0:T(8,128)(2,1)} %param.26) | copy-start | bytes 995332
  151.5 15.0 %collective-permute-start.7 = (bf16[2,384,161]{2,1,0:T(8,128)(2,1)S(1)}, bf16[2,384,161]{2,1,0:T(8,128)(2,1)S(1)}, u32[]{:S(2)}, u32[]{:S(2)}) collective-permute-start(bf16[2,384,161]{2,1,0:T(8,128)(2,1)S(1)} %get-tuple-element.16), channel_id=1, source_target_pairs={{4,0},{8,4},{12,8},{16,12},{20,16},{24,20},{28,24},{32,28},{36,32}... | collective-permute-start | bytes 741896 | tf_op jit(solution)/shard_map/ppermute | solution.py:23
  157.6 17.2 %collective-permute-start.6 = (bf16[2,384,161]{2,1,0:T(8,128)(2,1)S(1)}, bf16[2,384,161]{2,1,0:T(8,128)(2,1)S(1)}, u32[]{:S(2)}, u32[]{:S(2)}) collective-permute-start(bf16[2,384,161]{2,1,0:T(8,128)(2,1)S(1)} %get-tuple-element.15), channel_id=1, source_target_pairs={{0,4},{4,8},{8,12},{12,16},{16,20},{20,24},{24,28},{28,32},{32,36}... | collective-permute-start | bytes 741896 | tf_op jit(solution)/shard_map/ppermute | solution.py:20
  180.1 1.6 copy-start.14
where the time goes:
time: 184 us; the launch traced here: 182 us
  matrix products  54.8 us (30%)
  blocking collectives  49.3 us (27%)
  starting transfers between devices  31.7 us (17%)
  waiting for transfers between devices  28.7 us (16%)
  local copies, waits for them, and re-layouts  14.8 us (8%)
  other arithmetic  2.17 us (1%)
    dot_general x81, matrix products, causal_terms(): jnp.einsum('ok,fkr->for', weight_rows[time_tap, row_tap, column_tap], win...  49.7 us
    all_gather x4, blocking collectives, convolve(): complete = lax.all_gather(source, 'chan', axis=1, tiled=True)  32 us
    ppermute x4, starting transfers between devices, extended(): lax.ppermute(lax.slice_in_dim(block, 0, width, axis=dim), axis, backward)  23.8 us
    psum x2, blocking collectives, activate(): total_sq = lax.psum(squares, 'chan')  17.2 us
    ppermute x4, waiting for transfers between devices, extended(): lax.ppermute(lax.slice_in_dim(block, block.shape[dim] - width, None, axis...  15.2 us
    ppermute x4, waiting for transfers between devices, extended(): lax.ppermute(lax.slice_in_dim(block, 0, width, axis=dim), axis, backward)  13.5 us
    ppermute x4, starting transfers between devices, extended(): lax.ppermute(lax.slice_in_dim(block, block.shape[dim] - width, None, axis...  7.9 us
    dot_general x25, matrix products, upsample_terms(): jnp.einsum('ok,fkr->for', weight_rows[row_tap, column_tap], window, prefe...  5.11 us
  transfers between devices with their start and end apart: 8, of which 7 were waited for; matrix products, arithmetic and copies ran while one was open for 17% of the time, Pallas kernels for 0%

commit v1 on v0

v1 whole, which is shorter than its diff:
```python
import functools

import jax
import jax.numpy as jnp
from jax import lax
from jax.experimental import pallas as pl
from jax.experimental.pallas import tpu as pltpu
from jax.sharding import PartitionSpec as P

C = 384
W = 160
EPS = 1e-06
LANES = 256
GROUPS = 4
MESH = pl.DeviceIdType.MESH
LOW, OWN, HIGH = 0, 1, 2
F32 = jnp.float32
BF16 = jnp.bfloat16


def dot(a, b):
    return lax.dot_general(a, b, (((1,), (0,)), ((), ())), preferred_element_type=F32)


def padded(value, lanes=LANES):
    rows, count = value.shape
    return jnp.concatenate([value, jnp.zeros((rows, lanes - count), value.dtype)], axis=1)


def row_window(step, low, own, high, span):
    begin = span + (step - 1) * W - 1
    parts = []
    for piece, first in ((low, 0), (own, span), (high, 2 * span)):
        lo, hi = max(begin, first), min(begin + span + 2, first + span)
        if lo < hi:
            parts.append(piece[:, lo - first : hi - first])
    parts.append(jnp.zeros((low.shape[0], LANES - span - 2), low.dtype))
    return jnp.concatenate(parts, axis=1)


def body(
    tiles,
    span,
    latent,
    latent_cache,
    weight_in,
    bias_in,
    cache_a,
    gain_a,
    weight_a,
    bias_a,
    cache_b,
    gain_b,
    weight_b,
    bias_b,
    weight_up,
    bias_up,
    out,
    own_lat,
    lat,
    win,
    par,
    held_a,
    held_b,
    swap_a,
    swap_b,
    stem,
    maps,
    early,
    wa,
    wb,
    wu,
    up_left,
    spread,
    loc_sem,
    lat_send,
    lat_recv,
    par_send,
    par_recv,
    send_sem,
    recv_sem,
):
    tile = lax.axis_index("tile")
    chan = lax.axis_index("chan")
    mate = (tile, chan + 1 - 2 * lax.rem(chan, 2))
    far_chan = lax.rem(chan + 2, GROUPS)
    far = (tile, far_chan)
    mate_far_chan = lax.rem(mate[1] + 2, GROUPS)
    shifted = {d: lax.rem(tile + d + tiles, tiles) for d in (-2, -1, 1, 2)}
    right = (shifted[1], chan)
    left = (shifted[-1], chan)
    total = tiles * span
    start = tile * span

    def remote(src, dst, send, recv, device):
        return pltpu.make_async_remote_copy(
            src_ref=src,
            dst_ref=dst,
            send_sem=send,
            recv_sem=recv,
            device_id=device,
            device_id_type=MESH,
        )

    barrier = pltpu.get_barrier_semaphore()
    greeted = [mate, far]
    for d in (-2, -1, 1, 2):
        greeted += [(shifted[d], chan), (shifted[d], far_chan)]
    for device in greeted:
        pl.semaphore_signal(barrier, inc=1, device_id=device, device_id_type=MESH)

    local = [
        pltpu.make_async_copy(weight_a, wa, loc_sem.at[0]),
        pltpu.make_async_copy(weight_b, wb, loc_sem.at[1]),
        pltpu.make_async_copy(weight_up, wu, loc_sem.at[2]),
        pltpu.make_async_copy(cache_a, held_a.at[OWN, chan], loc_sem.at[3]),
        pltpu.make_async_copy(cache_b, held_b.at[OWN, chan], loc_sem.at[4]),
    ]
    for copy in local:
        copy.start()

    own_lat[...] = jnp.concatenate(
        [latent_cache[0].astype(F32), latent_cache[1].astype(F32), latent[0].astype(F32), latent[1].astype(F32)],
        axis=0,
    ).astype(BF16)
    win[chan] = jnp.concatenate(
        [
            weight_in[(a * 3 + b) * 3 + c].astype(F32)
            for b in range(3)
            for c in range(3)
            for a in range(3)
        ],
        axis=1,
    ).astype(BF16)
    par[chan] = jnp.concatenate(
        [
            padded(bias_in[...], 128),
            padded(gain_a[...], 128),
            padded(gain_b[...], 128),
            padded(bias_a[...], 128),
            padded(bias_b[...], 128),
            padded(bias_up[...], 128),
            jnp.zeros((2, 128), F32),
        ],
        axis=0,
    )
    pl.semaphore_wait(barrier, len(greeted))

    sends = []

    def go(copy):
        copy.start()
        sends.append(copy)

    lat[2, chan] = own_lat[...]
    index = 0
    for group in (chan, far_chan):
        for d in (-2, -1, 0, 1, 2):
            if d == 0 and group is chan:
                continue
            device = (tile if d == 0 else shifted[d], group)
            go(remote(own_lat, lat.at[2 - d, chan], lat_send.at[index], lat_recv.at[index], device))
            index += 1
    lat_count = index

    def par_copy(slot, group, device):
        go(remote(win.at[group], win.at[group], par_send.at[slot], par_recv.at[slot], device))
        go(remote(par.at[group], par.at[group], par_send.at[slot + 3], par_recv.at[slot + 3], device))

    par_copy(0, chan, far)
    par_copy(1, chan, mate)

    def exchange_copy(which, buf, number, group, slot, device, first=None):
        src = buf.at[OWN, group] if first is None else first
        return remote(
            src, buf.at[slot, group], send_sem.at[which, number], recv_sem.at[which, number], device
        )

    def send_own(which, buf, first=None):
        go(exchange_copy(which, buf, 0, chan, OWN, far, first))
        go(exchange_copy(which, buf, 2, chan, LOW, right, first))
        go(exchange_copy(which, buf, 3, chan, HIGH, left, first))
        go(exchange_copy(which, buf, 1, chan, OWN, mate, first))

    def landed(which, buf, number, slot, group):
        exchange_copy(which, buf, number, group, slot, mate).wait_recv()

    def pass_far(which, buf):
        landed(which, buf, 0, OWN, far_chan)
        go(exchange_copy(which, buf, 5, far_chan, LOW, right))
        go(exchange_copy(which, buf, 6, far_chan, HIGH, left))
        go(exchange_copy(which, buf, 4, far_chan, OWN, mate))

    def pass_rim(which, buf):
        for number, slot, group, onward in (
            (2, LOW, chan, 7),
            (3, HIGH, chan, 8),
            (5, LOW, far_chan, 9),
            (6, HIGH, far_chan, 10),
        ):
            landed(which, buf, number, slot, group)
            go(
                remote(
                    buf.at[slot, group],
                    buf.at[slot, group],
                    send_sem.at[which, onward],
                    recv_sem.at[which, onward],
                    mate,
                )
            )

    def take_mate(which, buf):
        landed(which, buf, 1, OWN, mate[1])
        landed(which, buf, 4, OWN, mate_far_chan)
        landed(which, buf, 7, LOW, mate[1])
        landed(which, buf, 8, HIGH, mate[1])
        landed(which, buf, 9, LOW, mate_far_chan)
        landed(which, buf, 10, HIGH, mate_far_chan)

    send_own(0, held_a, cache_a)
    send_own(1, held_b, cache_b)

    remote(win.at[chan], win.at[far_chan], par_send.at[0], par_recv.at[0], far).wait_recv()
    remote(par.at[chan], par.at[far_chan], par_send.at[3], par_recv.at[3], far).wait_recv()
    par_copy(2, far_chan, mate)
    for number in range(lat_count):
        remote(own_lat, lat.at[0, chan], lat_send.at[number], lat_recv.at[number], far).wait_recv()
    for slot, group in ((0, chan), (1, far_chan)):
        go(
            remote(
                lat.at[:, group],
                lat.at[:, group],
                lat_send.at[lat_count + slot],
                lat_recv.at[lat_count + slot],
                mate,
            )
        )
    pass_far(0, held_a)

    lane = lax.broadcasted_iota(jnp.int32, (1, LANES), 1)
    column = lax.rem(start + lane, W)
    inner_column = lax.rem(start + lane + (W - 1), W)
    first_column = column == 0
    last_column = column == W - 1

    def inside(step):
        cell = start + (step - 1) * W - 1 + lane
        return (cell >= 0) & (cell < total)

    remote(win.at[chan], win.at[mate[1]], par_send.at[1], par_recv.at[1], mate).wait_recv()
    remote(par.at[chan], par.at[mate[1]], par_send.at[4], par_recv.at[4], mate).wait_recv()
    remote(win.at[chan], win.at[mate_far_chan], par_send.at[2], par_recv.at[2], mate).wait_recv()
    remote(par.at[chan], par.at[mate_far_chan], par_send.at[5], par_recv.at[5], mate).wait_recv()
    columns = [par[g].T for g in range(GROUPS)]

    def full_column(number):
        return jnp.concatenate([part[: C // GROUPS, number : number + 1] for part in columns], axis=0)

    bias_in_column = full_column(0)
    gain_a_column = full_column(1)
    gain_b_column = full_column(2)
    own_columns = par[chan].T
    bias_a_column = own_columns[: C // GROUPS, 3:4]
    bias_b_column = own_columns[: C // GROUPS, 4:5]
    bias_up_column = own_columns[: C // GROUPS // 2, 5:6]

    for slot, group in ((0, mate[1]), (1, mate_far_chan)):
        remote(
            lat.at[:, group],
            lat.at[:, group],
            lat_send.at[lat_count + slot],
            lat_recv.at[lat_count + slot],
            mate,
        ).wait_recv()
    depth = GROUPS * own_lat.shape[0]
    place = lax.broadcasted_iota(jnp.int32, (depth, depth), 0)
    taken = lax.broadcasted_iota(jnp.int32, (depth, depth), 1)
    quarter = depth // 4
    small = quarter // GROUPS
    source = lax.rem(place, quarter) // small * quarter + place // quarter * small + lax.rem(place, small)
    order = jnp.where(source == taken, 1.0, 0.0).astype(BF16)
    wide = jnp.concatenate([dot(order, lat[d].reshape(depth, span)) for d in range(5)], axis=1)
    cell = start - 2 * span + lax.broadcasted_iota(jnp.int32, (1, 5 * span), 1)
    wide = jnp.where((cell >= 0) & (cell < total), wide, 0.0)
    views = {}
    for row in range(5):
        for tap in range(3):
            begin = 2 * span + (row - 2) * W + tap - 2
            view = padded(wide[:, begin : begin + span + 2])
            if tap == 0:
                view = jnp.where(inner_column == 0, 0.0, view)
            if tap == 2:
                view = jnp.where(inner_column == W - 1, 0.0, view)
            views[row, tap] = view.astype(BF16)
    stem_left = win[...].reshape(C, win.shape[2])

    def activate(values, gain_column, step):
        values = values.astype(F32)
        scale = lax.rsqrt(jnp.sum(values * values, axis=0, keepdims=True) * (1.0 / C) + EPS)
        values = values * scale * gain_column
        values = values / (1.0 + jnp.exp(-values))
        return jnp.where(inside(step), values, 0.0).astype(BF16)

    for frame in range(2):
        for step in range(3):
            right_side = jnp.concatenate(
                [
                    views[step + b, c][frame * quarter : (frame + 3) * quarter]
                    for b in range(3)
                    for c in range(3)
                ],
                axis=0,
            )
            values = (dot(stem_left, right_side) + bias_in_column).astype(BF16)
            if step == 1:
                stem[frame] = values.reshape(GROUPS, C // GROUPS, LANES)
            maps[2 + frame, step] = activate(values, gain_a_column, step)

    pass_rim(0, held_a)
    pass_far(1, held_b)
    local[3].wait()
    take_mate(0, held_a)

    def windows(buf, frame, step):
        pieces = [buf[slot, :, frame].reshape(C, span) for slot in (LOW, OWN, HIGH)]
        return row_window(step, *pieces, span)

    def load_history(buf):
        for frame in range(2):
            for step in range(3):
                values = windows(buf, frame, step)
                maps[frame, step] = jnp.where(inside(step), values, jnp.zeros_like(values))

    def taps(weight, frame, time_taps):
        acc = None
        for a in time_taps:
            for b in range(3):
                term = dot(weight[a * 3 + b], maps[frame + a, b])
                acc = term if acc is None else acc + term
        return acc

    def finish(acc, frame, bias_column, added):
        width = C // GROUPS
        middle = acc[width : 2 * width]
        if added is not None:
            middle = middle + added.astype(F32)
        result = jnp.where(first_column, 0.0, acc[:width])
        result = result + pltpu.roll(middle, LANES - 1, 1)
        result = result + jnp.where(last_column, 0.0, pltpu.roll(acc[2 * width :], LANES - 2, 1))
        return (result + bias_column).astype(BF16)[:, :span]

    load_history(held_a)
    local[0].wait()
    for frame in range(2):
        swap_a[OWN, chan, frame] = finish(taps(wa, frame, (0, 1, 2)), frame, bias_a_column, None)
    send_own(2, swap_a)

    pass_rim(1, held_b)
    local[4].wait()
    take_mate(1, held_b)
    load_history(held_b)
    local[1].wait()
    early[0] = taps(wb, 0, (0, 1))
    early[1] = taps(wb, 1, (0,))

    pass_far(2, swap_a)
    pass_rim(2, swap_a)
    take_mate(2, swap_a)
    for frame in range(2):
        for step in range(3):
            maps[2 + frame, step] = activate(windows(swap_a, frame, step), gain_b_column, step)
    for frame in range(2):
        acc = early[frame] + taps(wb, frame, (2,) if frame == 0 else (1, 2))
        swap_b[OWN, chan, frame] = finish(acc, frame, bias_b_column, stem[frame, chan])
    send_own(3, swap_b)

    local[2].wait()
    outs = C // GROUPS // 2
    row_sets = (((0,), (1, 2)), ((0, 1), (2,)))
    column_sets = ((0,), (1, 2), (0, 1), (2,))
    for p in range(2):
        for half in range(2):
            for block in range(4):
                summed = None
                for b in row_sets[p][half]:
                    for c in column_sets[block]:
                        term = wu[b * 3 + c].astype(F32)
                        summed = term if summed is None else summed + term
                up_left[p, block * outs : (block + 1) * outs, half * C : (half + 1) * C] = summed.astype(
                    BF16
                )
    half_lanes = LANES // 2
    into = lax.broadcasted_iota(jnp.int32, (4 * half_lanes, 4 * half_lanes), 1)
    whence = lax.broadcasted_iota(jnp.int32, (4 * half_lanes, 4 * half_lanes), 0)
    wanted = lax.rem(whence, half_lanes) * 4 + whence // half_lanes
    spread[...] = jnp.where(into == wanted, 1.0, 0.0).astype(BF16)

    pass_far(3, swap_b)
    pass_rim(3, swap_b)
    take_mate(3, swap_b)
    pieces = []
    for frame in range(2):
        for step in range(3):
            values = windows(swap_b, frame, step)
            maps[frame, step] = jnp.where(inside(step), values, jnp.zeros_like(values))
        quarters = []
        for p in range(2):
            acc = dot(up_left[p], maps[frame, p : p + 2].reshape(2 * C, LANES))
            even = jnp.where(first_column, 0.0, acc[:outs]) + pltpu.roll(acc[outs : 2 * outs], LANES - 1, 1)
            odd = pltpu.roll(acc[2 * outs : 3 * outs], LANES - 1, 1) + jnp.where(
                last_column, 0.0, pltpu.roll(acc[3 * outs :], LANES - 2, 1)
            )
            quarters += [(even + bias_up_column).astype(BF16), (odd + bias_up_column).astype(BF16)]
        pieces.append(quarters)
    for frame in range(2):
        quarters = pieces[frame]
        for side in range(2):
            joined = jnp.concatenate(
                [part[:, side * half_lanes : (side + 1) * half_lanes] for part in quarters], axis=1
            )
            woven = dot(joined, spread[...]).astype(BF16)
            first = side * 4 * half_lanes
            count = min(4 * half_lanes, 4 * span - first)
            out[frame, :, first : first + count] = woven[:, :count]

    for copy in sends:
        copy.wait_send()


def shards(tiles, *operands):
    (
        latent,
        latent_cache,
        weight_in,
        bias_in,
        cache_a,
        gain_a,
        weight_a,
        bias_a,
        cache_b,
        gain_b,
        weight_b,
        bias_b,
        weight_up,
        bias_up,
    ) = operands
    span = latent.shape[2]
    width = C // GROUPS
    small = latent.shape[1]
    depth = 27 * weight_in.shape[4]
    vmem = pl.BlockSpec(memory_space=pltpu.VMEM)
    hbm = pl.BlockSpec(memory_space=pl.ANY)
    block = pltpu.VMEM((3, GROUPS, 2, width, span), BF16)
    dma = pltpu.SemaphoreType.DMA
    row = lambda vector: vector.reshape(1, -1)
    return pl.pallas_call(
        functools.partial(body, tiles, span),
        out_shape=jax.ShapeDtypeStruct((2, width // 2, 4 * span), BF16),
        in_specs=[vmem, vmem, vmem, vmem, hbm, vmem, hbm, vmem, hbm, vmem, hbm, vmem, hbm, vmem],
        out_specs=vmem,
        scratch_shapes=[
            pltpu.VMEM((4 * small, span), BF16),
            pltpu.VMEM((5, GROUPS, 4 * small, span), BF16),
            pltpu.VMEM((GROUPS, width, depth), BF16),
            pltpu.VMEM((GROUPS, 8, 128), F32),
            block,
            block,
            block,
            block,
            pltpu.VMEM((2, GROUPS, width, LANES), BF16),
            pltpu.VMEM((4, 3, C, LANES), BF16),
            pltpu.VMEM((2, 3 * width, LANES), F32),
            pltpu.VMEM((9, 3 * width, C), BF16),
            pltpu.VMEM((9, 3 * width, C), BF16),
            pltpu.VMEM((9, width // 2, C), BF16),
            pltpu.VMEM((2, 4 * width // 2, 2 * C), BF16),
            pltpu.VMEM((2 * LANES, 2 * LANES), BF16),
            dma((5,)),
            dma((11,)),
            dma((11,)),
            dma((6,)),
            dma((6,)),
            dma((4, 11)),
            dma((4, 11)),
        ],
        compiler_params=pltpu.CompilerParams(
            collective_id=0, has_side_effects=True, vmem_limit_bytes=56 << 20
        ),
    )(
        latent,
        latent_cache,
        weight_in.reshape(27, width, -1),
        row(bias_in),
        cache_a,
        row(gain_a),
        weight_a.reshape(9, 3 * width, C),
        row(bias_a),
        cache_b,
        row(gain_b),
        weight_b.reshape(9, 3 * width, C),
        row(bias_b),
        weight_up.reshape(9, width // 2, C),
        row(bias_up),
    )


def solution(mesh):
    placed = (
        P(None, "chan", "tile"),
        P(None, "chan", "tile"),
        P(None, None, None, "chan", None),
        P("chan"),
        P(None, "chan", "tile"),
        P("chan"),
        P(None, None, None, "chan", None),
        P("chan"),
        P(None, "chan", "tile"),
        P("chan"),
        P(None, None, None, "chan", None),
        P("chan"),
        P(None, None, "chan", None),
        P("chan"),
    )
    return jax.shard_map(
        functools.partial(shards, mesh.shape["tile"]),
        mesh=mesh,
        in_specs=placed,
        out_specs=P(None, "chan", "tile"),
        check_vma=False,
    )
```

time: 184 us -> 69.3 us (0.38)
  the two profiles are of different devices: /device:TPU:128 before, /device:TPU:17 now
where the time goes in v1:
time: 69.3 us; the launch traced here: 69.1 us
  Pallas kernels  65.5 us (95%)
  local copies, waits for them, and re-layouts  3.6 us (5%)
    pallas_call x1, Pallas kernels, shards(): pl.pallas_call(functools.partial(body, tiles, span), out_shape=jax.ShapeD...  65.5 us
    unnamed x2, local copies, waits for them, and re-layouts  3.6 us

profile of v1, /device:TPU:17, one launch (start us, length us, event | category | flops | bytes accessed | tf_op | source)
XLA Modules:
  0.0 69.1 jit_solution(989859679545082786)
XLA Ops:
  0.0 2.0 %copy.15 = bf16[3,3,3,96,16]{4,3,2,1,0:T(8,128)(2,1)} copy(bf16[3,3,3,96,16]{3,4,2,1,0:T(8,128)(2,1)} %param.16) | data formatting | bytes 165888 | tf_op args[2]
  2.0 65.5 %shard_map.136 = bf16[2,48,900]{2,1,0:T(8,128)(2,1)} custom-call(bf16[2,4,225]{2,1,0:T(4,128)(2,1)} %latent.1, bf16[2,4,225]{2,1,0:T(4,128)(2,1)} %latent_cache.1, bf16[27,96,16]{2,1,0:T(8,128)(2,1)} %bitcast.10, f32[1,96]{1,0:T(1,128)} %bitcast.14, bf16[2,96,225]{2,1,0:T(8,128)(2,1)} %cache_a.1, f32[1,96]{1,0:T(1,128)} %bitcast.15, ...), custom_call_target="tpu_custom_call" | custom-call | tf_op jit(solution)/shard_map/pallas_call | solution.py:456
  67.5 1.6 %copy.17 = bf16[2,48,900]{2,1,0:T(8,128)(2,1)} copy(bf16[2,48,900]{2,1,0:T(8,128)(2,1)} %shard_map.136) | data formatting | bytes 345600

commit v2 on v1

v2 whole, which is shorter than its diff:
```python
import functools

import jax
import jax.numpy as jnp
from jax import lax
from jax.experimental import pallas as pl
from jax.experimental.pallas import tpu as pltpu
from jax.sharding import PartitionSpec as P

C = 384
W = 160
EPS = 1e-06
LANES = 256
GROUPS = 4
MESH = pl.DeviceIdType.MESH
LOW, HIGH = 0, 1
F32 = jnp.float32
BF16 = jnp.bfloat16


def dot(a, b):
    return lax.dot_general(a, b, (((1,), (0,)), ((), ())), preferred_element_type=F32)


def padded(value, lanes=LANES):
    rows, count = value.shape
    return jnp.concatenate([value, jnp.zeros((rows, lanes - count), value.dtype)], axis=1)


def rim_packs(first, second, span):
    zeros = lambda count: jnp.zeros((first.shape[0], count), first.dtype)
    last = span - W - 1
    rest = W + 1 - 128
    low = jnp.concatenate(
        [
            first[:, last : last + 128],
            second[:, last : last + 128],
            first[:, span - rest :],
            zeros(64 - rest),
            second[:, span - rest :],
            zeros(64 - rest),
        ],
        axis=1,
    )
    head = 128 - (span - W + 1)
    tail = W + 1 - head
    high = jnp.concatenate(
        [
            first[:, head : W + 1],
            zeros(128 - tail),
            second[:, head : W + 1],
            zeros(128 - tail),
            zeros(64 - head),
            second[:, :head],
            zeros(64 - head),
            first[:, :head],
        ],
        axis=1,
    )
    return low, high


def row_windows(frame, low, own, high, span):
    zeros = jnp.zeros((own.shape[0], LANES - span - 2), own.dtype)
    rest = W + 1 - 128
    head = 128 - (span - W + 1)
    tail = W + 1 - head
    at_low = 256 + 64 * frame
    at_high = 256 + 64 * (2 - frame) - head
    return (
        jnp.concatenate(
            [
                low[:, 128 * frame : 128 * frame + 128],
                low[:, at_low : at_low + rest],
                own[:, : span + 1 - W],
                zeros,
            ],
            axis=1,
        ),
        jnp.concatenate(
            [low[:, at_low + rest - 1 : at_low + rest], own, high[:, at_high : at_high + 1], zeros], axis=1
        ),
        jnp.concatenate(
            [
                own[:, W - 1 :],
                high[:, at_high : at_high + head],
                high[:, 128 * frame : 128 * frame + tail],
                zeros,
            ],
            axis=1,
        ),
    )


def body(
    tiles,
    span,
    latent,
    latent_cache,
    weight_in,
    bias_in,
    cache_a,
    gain_a,
    weight_a,
    bias_a,
    cache_b,
    gain_b,
    weight_b,
    bias_b,
    weight_up,
    bias_up,
    out,
    own_lat,
    lat,
    win,
    par,
    held_a,
    held_a_rim,
    held_b,
    held_b_rim,
    swap_a,
    swap_a_rim,
    swap_b,
    swap_b_rim,
    packs,
    stem,
    maps,
    early,
    wa,
    wb,
    wu,
    up_left,
    spread,
    loc_sem,
    lat_send,
    lat_recv,
    par_send,
    par_recv,
    send_sem,
    recv_sem,
):
    tile = lax.axis_index("tile")
    chan = lax.axis_index("chan")
    mate = (tile, chan + 1 - 2 * lax.rem(chan, 2))
    far_chan = lax.rem(chan + 2, GROUPS)
    far = (tile, far_chan)
    core = lax.rem(chan, 2)
    here = 2 * core + chan // 2
    there = 2 * core + far_chan // 2
    both = pl.ds(2 * core, 2)
    mates = pl.ds(2 - 2 * core, 2)
    shifted = {d: lax.rem(tile + d + tiles, tiles) for d in (-2, -1, 1, 2)}
    right = (shifted[1], chan)
    left = (shifted[-1], chan)
    width = C // GROUPS
    total = tiles * span
    start = tile * span

    def remote(src, dst, send, recv, device):
        return pltpu.make_async_remote_copy(
            src_ref=src,
            dst_ref=dst,
            send_sem=send,
            recv_sem=recv,
            device_id=device,
            device_id_type=MESH,
        )

    barrier = pltpu.get_barrier_semaphore()
    near = {d: (tile + d >= 0) & (tile + d < tiles) for d in (-2, -1, 1, 2)}
    met = 2
    for d in (-2, -1, 1, 2):
        met = met + 2 * near[d].astype(jnp.int32)

        @pl.when(near[d])
        def _(d=d):
            for group in (chan, far_chan):
                device = (shifted[d], group)
                pl.semaphore_signal(barrier, inc=1, device_id=device, device_id_type=MESH)

    for device in (mate, far):
        pl.semaphore_signal(barrier, inc=1, device_id=device, device_id_type=MESH)

    local = [
        pltpu.make_async_copy(weight_a, wa, loc_sem.at[0]),
        pltpu.make_async_copy(weight_b, wb, loc_sem.at[1]),
        pltpu.make_async_copy(weight_up, wu, loc_sem.at[2]),
        pltpu.make_async_copy(cache_a, held_a.at[here], loc_sem.at[3]),
        pltpu.make_async_copy(cache_b, held_b.at[here], loc_sem.at[4]),
    ]
    for number in (3, 4, 0, 1, 2):
        local[number].start()

    def pack(which, buf, waited=None):
        if waited is not None:
            local[waited].wait()
        packs[which, 0], packs[which, 1] = rim_packs(buf[here, 0], buf[here, 1], span)

    own_lat[...] = jnp.concatenate(
        [latent_cache[0].astype(F32), latent_cache[1].astype(F32), latent[0].astype(F32), latent[1].astype(F32)],
        axis=0,
    ).astype(BF16)
    taps_first = jnp.concatenate(
        [weight_in[(a * 3 + b) * 3 + c].astype(F32) for b in range(3) for c in range(3) for a in range(3)],
        axis=0,
    )
    vectors = jnp.concatenate([bias_in[...], gain_a[...], gain_b[...]], axis=0)
    first = vectors.astype(BF16).astype(F32)
    second = (vectors - first).astype(BF16).astype(F32)
    third = (vectors - first - second).astype(BF16).astype(F32)
    rows = jnp.concatenate([taps_first, first, second, third, jnp.zeros((7, width), F32)], axis=0)
    win[here] = rows.T.astype(BF16)
    own_rows = jnp.concatenate([bias_a[...], bias_b[...], jnp.zeros((6, width), F32)], axis=0)
    par[...] = padded(own_rows, 128)
    par[2:3] = padded(bias_up[...], 128)
    pack(0, held_a, 3)
    pack(1, held_b, 4)
    pl.semaphore_wait(barrier, met)

    sends = []

    def guarded(condition, act):
        if condition is None:
            act()
        else:
            pl.when(condition)(act)

    def go(copy, condition=None):
        guarded(condition, copy.start)
        sends.append((condition, copy))

    lat[here, 2] = own_lat[...]
    index = 0
    lat_waits = []
    for group in (chan, far_chan):
        for d in (-2, -1, 0, 1, 2):
            if d == 0 and group is chan:
                continue
            device = (tile if d == 0 else shifted[d], group)
            copy = remote(own_lat, lat.at[here, 2 - d], lat_send.at[index], lat_recv.at[index], device)
            go(copy, near.get(d))
            lat_waits.append((near.get(-d), copy))
            index += 1
    lat_count = index
    go(remote(win.at[here], win.at[here], par_send.at[0], par_recv.at[0], far))

    def exchange_copy(which, src, dst, number, device):
        return remote(src, dst, send_sem.at[which, number], recv_sem.at[which, number], device)

    def send_own(which, own, rim):
        low = packs.at[which, 0]
        high = packs.at[which, 1]
        go(exchange_copy(which, low, rim.at[here, LOW], 4, (shifted[1], far_chan)), near[1])
        go(exchange_copy(which, high, rim.at[here, HIGH], 5, (shifted[-1], far_chan)), near[-1])
        go(exchange_copy(which, low, rim.at[here, LOW], 2, right), near[1])
        go(exchange_copy(which, high, rim.at[here, HIGH], 3, left), near[-1])
        go(exchange_copy(which, own.at[here], own.at[here], 1, far))

    def pass_on(which, own, rim):
        for numbers, onward, refs, ref in (
            ((1,), 6, (own.at[there],), own.at[both]),
            ((2, 3), 7, (rim.at[here, LOW], rim.at[here, HIGH]), rim.at[here]),
            ((4, 5), 8, (rim.at[there, LOW], rim.at[there, HIGH]), rim.at[there]),
        ):
            for number, landed in zip(numbers, refs):
                copy = exchange_copy(which, landed, landed, number, mate)
                guarded(None if number == 1 else near[1 if number % 2 else -1], copy.wait_recv)
            go(exchange_copy(which, ref, ref, onward, mate))

    def take_mate(which, own, rim):
        for number, ref in ((6, own.at[mates]), (7, rim.at[here]), (8, rim.at[there])):
            exchange_copy(which, ref, ref, number, mate).wait_recv()

    send_own(0, held_a, held_a_rim)

    remote(win.at[here], win.at[there], par_send.at[0], par_recv.at[0], far).wait_recv()
    go(remote(win.at[both], win.at[both], par_send.at[1], par_recv.at[1], mate))
    for condition, copy in lat_waits:
        guarded(condition, copy.wait_recv)
    go(remote(lat.at[both], lat.at[both], lat_send.at[lat_count], lat_recv.at[lat_count], mate))
    pass_on(0, held_a, held_a_rim)
    send_own(1, held_b, held_b_rim)

    lane = lax.broadcasted_iota(jnp.int32, (1, LANES), 1)
    column = lax.rem(start + lane, W)
    inner_column = lax.rem(start + lane + (W - 1), W)
    first_column = column == 0
    last_column = column == W - 1

    def inside(step):
        cell = start + (step - 1) * W - 1 + lane
        return (cell >= 0) & (cell < total)

    remote(win.at[both], win.at[mates], par_send.at[1], par_recv.at[1], mate).wait_recv()
    order = (0, 2, 1, 3)
    depth = 27 * weight_in.shape[1]
    stem_left = jnp.concatenate([win[number] for number in order], axis=0)

    def full_column(number):
        parts = [stem_left[:, depth + number + 3 * k :][:, :1].astype(F32) for k in range(3)]
        return parts[0] + parts[1] + parts[2]

    bias_in_column = full_column(0)
    gain_a_column = full_column(1)
    gain_b_column = full_column(2)
    own_columns = par[...].T
    bias_a_column = own_columns[:width, 0:1]
    bias_b_column = own_columns[:width, 1:2]
    bias_up_column = own_columns[: width // 2, 2:3]
    stem_left = stem_left[:, :depth]

    remote(lat.at[both], lat.at[mates], lat_send.at[lat_count], lat_recv.at[lat_count], mate).wait_recv()
    depth = GROUPS * own_lat.shape[0]
    place = lax.broadcasted_iota(jnp.int32, (depth, depth), 0)
    taken = lax.broadcasted_iota(jnp.int32, (depth, depth), 1)
    quarter = depth // 4
    small = quarter // GROUPS
    source = lax.rem(place, quarter) // small * quarter + place // quarter * small + lax.rem(place, small)
    sorter = jnp.where(source == taken, 1.0, 0.0).astype(BF16)
    wide = jnp.concatenate(
        [dot(sorter, jnp.concatenate([lat[number, d] for number in order], axis=0)) for d in range(5)], axis=1
    )
    cell = start - 2 * span + lax.broadcasted_iota(jnp.int32, (1, 5 * span), 1)
    wide = jnp.where((cell >= 0) & (cell < total), wide, 0.0)
    views = {}
    for row in range(5):
        for tap in range(3):
            begin = 2 * span + (row - 2) * W + tap - 2
            view = padded(wide[:, begin : begin + span + 2])
            if tap == 0:
                view = jnp.where(inner_column == 0, 0.0, view)
            if tap == 2:
                view = jnp.where(inner_column == W - 1, 0.0, view)
            views[row, tap] = view.astype(BF16)

    def activate(values, gain_column, step):
        values = values.astype(F32)
        scale = lax.rsqrt(jnp.sum(values * values, axis=0, keepdims=True) * (1.0 / C) + EPS)
        values = values * scale * gain_column
        values = values / (1.0 + jnp.exp(-values))
        return jnp.where(inside(step), values, 0.0).astype(BF16)

    for frame in range(2):
        for step in range(3):
            right_side = jnp.concatenate(
                [
                    views[step + b, c][frame * quarter : (frame + 3) * quarter]
                    for b in range(3)
                    for c in range(3)
                ],
                axis=0,
            )
            values = (dot(stem_left, right_side) + bias_in_column).astype(BF16)
            if step == 1:
                stem[frame] = values.reshape(GROUPS, C // GROUPS, LANES)
            maps[2 + frame, step] = activate(values, gain_a_column, step)

    take_mate(0, held_a, held_a_rim)

    def windows(own, rim, frame):
        low, high = (jnp.concatenate([rim[number, side] for number in order], axis=0) for side in (LOW, HIGH))
        middle = jnp.concatenate([own[number, frame] for number in order], axis=0)
        return row_windows(frame, low, middle, high, span)

    def load_windows(own, rim):
        for frame in range(2):
            for step, values in enumerate(windows(own, rim, frame)):
                maps[frame, step] = jnp.where(inside(step), values, jnp.zeros_like(values))

    def taps(weight, frame, time_taps):
        acc = None
        for a in time_taps:
            for b in range(3):
                term = dot(weight[a * 3 + b], maps[frame + a, b])
                acc = term if acc is None else acc + term
        return acc

    def finish(acc, frame, bias_column, added):
        middle = acc[width : 2 * width]
        if added is not None:
            middle = middle + added.astype(F32)
        result = jnp.where(first_column, 0.0, acc[:width])
        result = result + pltpu.roll(middle, LANES - 1, 1)
        result = result + jnp.where(last_column, 0.0, pltpu.roll(acc[2 * width :], LANES - 2, 1))
        return (result + bias_column).astype(BF16)[:, :span]

    load_windows(held_a, held_a_rim)
    local[0].wait()
    for frame in range(2):
        swap_a[here, frame] = finish(taps(wa, frame, (0, 1, 2)), frame, bias_a_column, None)
    pack(2, swap_a)
    send_own(2, swap_a, swap_a_rim)

    pass_on(1, held_b, held_b_rim)
    take_mate(1, held_b, held_b_rim)
    load_windows(held_b, held_b_rim)
    local[1].wait()
    early[0] = taps(wb, 0, (0, 1))
    early[1] = taps(wb, 1, (0,))

    pass_on(2, swap_a, swap_a_rim)
    take_mate(2, swap_a, swap_a_rim)
    for frame in range(2):
        for step, values in enumerate(windows(swap_a, swap_a_rim, frame)):
            maps[2 + frame, step] = activate(values, gain_b_column, step)
    for frame in range(2):
        acc = early[frame] + taps(wb, frame, (2,) if frame == 0 else (1, 2))
        swap_b[here, frame] = finish(acc, frame, bias_b_column, stem[frame, chan])
    pack(3, swap_b)
    send_own(3, swap_b, swap_b_rim)

    local[2].wait()
    outs = C // GROUPS // 2
    row_sets = (((0,), (1, 2)), ((0, 1), (2,)))
    column_sets = ((0,), (1, 2), (0, 1), (2,))
    for p in range(2):
        for half in range(2):
            for block in range(4):
                summed = None
                for b in row_sets[p][half]:
                    for c in column_sets[block]:
                        term = wu[b * 3 + c].astype(F32)
                        summed = term if summed is None else summed + term
                up_left[p, block * outs : (block + 1) * outs, half * C : (half + 1) * C] = summed.astype(
                    BF16
                )
    half_lanes = LANES // 2
    into = lax.broadcasted_iota(jnp.int32, (4 * half_lanes, 4 * half_lanes), 1)
    whence = lax.broadcasted_iota(jnp.int32, (4 * half_lanes, 4 * half_lanes), 0)
    wanted = lax.rem(whence, half_lanes) * 4 + whence // half_lanes
    spread[...] = jnp.where(into == wanted, 1.0, 0.0).astype(BF16)

    pass_on(3, swap_b, swap_b_rim)
    take_mate(3, swap_b, swap_b_rim)
    load_windows(swap_b, swap_b_rim)
    pieces = []
    for frame in range(2):
        quarters = []
        for p in range(2):
            acc = dot(up_left[p], maps[frame, p : p + 2].reshape(2 * C, LANES))
            even = jnp.where(first_column, 0.0, acc[:outs]) + pltpu.roll(acc[outs : 2 * outs], LANES - 1, 1)
            odd = pltpu.roll(acc[2 * outs : 3 * outs], LANES - 1, 1) + jnp.where(
                last_column, 0.0, pltpu.roll(acc[3 * outs :], LANES - 2, 1)
            )
            quarters += [(even + bias_up_column).astype(BF16), (odd + bias_up_column).astype(BF16)]
        pieces.append(quarters)
    for frame in range(2):
        quarters = pieces[frame]
        for side in range(2):
            joined = jnp.concatenate(
                [part[:, side * half_lanes : (side + 1) * half_lanes] for part in quarters], axis=1
            )
            woven = dot(joined, spread[...]).astype(BF16)
            first = side * 4 * half_lanes
            count = min(4 * half_lanes, 4 * span - first)
            out[frame, :, first : first + count] = woven[:, :count]

    for condition, copy in sends:
        guarded(condition, copy.wait_send)


def shards(tiles, *operands):
    (
        latent,
        latent_cache,
        weight_in,
        bias_in,
        cache_a,
        gain_a,
        weight_a,
        bias_a,
        cache_b,
        gain_b,
        weight_b,
        bias_b,
        weight_up,
        bias_up,
    ) = operands
    span = latent.shape[2]
    width = C // GROUPS
    small = latent.shape[1]
    depth = 27 * weight_in.shape[4]
    vmem = pl.BlockSpec(memory_space=pltpu.VMEM)
    hbm = pl.BlockSpec(memory_space=pl.ANY)
    block = pltpu.VMEM((GROUPS, 2, width, span), BF16)
    rim = pltpu.VMEM((GROUPS, 2, width, 384), BF16)
    dma = pltpu.SemaphoreType.DMA
    row = lambda vector: vector.reshape(1, -1)
    return pl.pallas_call(
        functools.partial(body, tiles, span),
        out_shape=jax.ShapeDtypeStruct((2, width // 2, 4 * span), BF16),
        in_specs=[vmem, vmem, vmem, vmem, hbm, vmem, hbm, vmem, hbm, vmem, hbm, vmem, hbm, vmem],
        out_specs=vmem,
        scratch_shapes=[
            pltpu.VMEM((4 * small, span), BF16),
            pltpu.VMEM((GROUPS, 5, 4 * small, span), BF16),
            pltpu.VMEM((GROUPS, width, depth + 16), BF16),
            pltpu.VMEM((8, 128), F32),
            block,
            rim,
            block,
            rim,
            block,
            rim,
            block,
            rim,
            pltpu.VMEM((4, 2, width, 384), BF16),
            pltpu.VMEM((2, GROUPS, width, LANES), BF16),
            pltpu.VMEM((4, 3, C, LANES), BF16),
            pltpu.VMEM((2, 3 * width, LANES), F32),
            pltpu.VMEM((9, 3 * width, C), BF16),
            pltpu.VMEM((9, 3 * width, C), BF16),
            pltpu.VMEM((9, width // 2, C), BF16),
            pltpu.VMEM((2, 4 * width // 2, 2 * C), BF16),
            pltpu.VMEM((2 * LANES, 2 * LANES), BF16),
            dma((5,)),
            dma((10,)),
            dma((10,)),
            dma((2,)),
            dma((2,)),
            dma((4, 9)),
            dma((4, 9)),
        ],
        compiler_params=pltpu.CompilerParams(
            collective_id=0, has_side_effects=True, vmem_limit_bytes=56 << 20
        ),
    )(
        latent,
        latent_cache,
        weight_in.swapaxes(3, 4).reshape(27, -1, width),
        row(bias_in),
        cache_a,
        row(gain_a),
        weight_a.reshape(9, 3 * width, C),
        row(bias_a),
        cache_b,
        row(gain_b),
        weight_b.reshape(9, 3 * width, C),
        row(bias_b),
        weight_up.reshape(9, width // 2, C),
        row(bias_up),
    )


def solution(mesh):
    placed = (
        P(None, "chan", "tile"),
        P(None, "chan", "tile"),
        P(None, None, None, "chan", None),
        P("chan"),
        P(None, "chan", "tile"),
        P("chan"),
        P(None, None, None, "chan", None),
        P("chan"),
        P(None, "chan", "tile"),
        P("chan"),
        P(None, None, None, "chan", None),
        P("chan"),
        P(None, None, "chan", None),
        P("chan"),
    )
    return jax.shard_map(
        functools.partial(shards, mesh.shape["tile"]),
        mesh=mesh,
        in_specs=placed,
        out_specs=P(None, "chan", "tile"),
        check_vma=False,
    )
```

time: 69.3 us -> 48.4 us (0.70)
  the two profiles are of different devices: /device:TPU:17 before, /device:TPU:97 now
where the time goes in v2:
time: 48.4 us; the launch traced here: 48.2 us
  Pallas kernels  46.6 us (96%)
  local copies, waits for them, and re-layouts  1.62 us (3%)
    pallas_call x1, Pallas kernels, shards(): pl.pallas_call(functools.partial(body, tiles, span), out_shape=jax.ShapeD...  46.6 us
    unnamed x1, local copies, waits for them, and re-layouts  1.62 us

profile of v2, /device:TPU:97, one launch (start us, length us, event | category | flops | bytes accessed | tf_op | source)
XLA Modules:
  0.0 48.2 jit_solution(18261755298748761957)
XLA Ops:
  0.0 46.6 %shard_map.136 = bf16[2,48,900]{2,1,0:T(8,128)(2,1)} custom-call(bf16[2,4,225]{2,1,0:T(4,128)(2,1)} %latent.1, bf16[2,4,225]{2,1,0:T(4,128)(2,1)} %latent_cache.1, bf16[27,16,96]{2,1,0:T(8,128)(2,1)} %bitcast.15, f32[1,96]{1,0:T(1,128)} %bitcast.16, bf16[2,96,225]{2,1,0:T(8,128)(2,1)} %cache_a.1, f32[1,96]{1,0:T(1,128)} %bitcast.17, ...), custom_call_target="tpu_custom_call" | custom-call | tf_op jit(solution)/shard_map/pallas_call | solution.py:489
  46.6 1.6 %copy.16 = bf16[2,48,900]{2,1,0:T(8,128)(2,1)} copy(bf16[2,48,900]{2,1,0:T(8,128)(2,1)} %shard_map.136) | data formatting | bytes 345600

commit v3 on v2

--- a/solution.py
+++ b/solution.py
@@ -169,7 +169,7 @@
     barrier = pltpu.get_barrier_semaphore()
     near = {d: (tile + d >= 0) & (tile + d < tiles) for d in (-2, -1, 1, 2)}
     met = 2
-    for d in (-2, -1, 1, 2):
+    for d in (-1, 1):
         met = met + 2 * near[d].astype(jnp.int32)
 
         @pl.when(near[d])
@@ -210,11 +210,7 @@
     third = (vectors - first - second).astype(BF16).astype(F32)
     rows = jnp.concatenate([taps_first, first, second, third, jnp.zeros((7, width), F32)], axis=0)
     win[here] = rows.T.astype(BF16)
-    own_rows = jnp.concatenate([bias_a[...], bias_b[...], jnp.zeros((6, width), F32)], axis=0)
-    par[...] = padded(own_rows, 128)
-    par[2:3] = padded(bias_up[...], 128)
     pack(0, held_a, 3)
-    pack(1, held_b, 4)
     pl.semaphore_wait(barrier, met)
 
     sends = []
@@ -230,18 +226,12 @@
         sends.append((condition, copy))
 
     lat[here, 2] = own_lat[...]
-    index = 0
     lat_waits = []
-    for group in (chan, far_chan):
-        for d in (-2, -1, 0, 1, 2):
-            if d == 0 and group is chan:
-                continue
-            device = (tile if d == 0 else shifted[d], group)
-            copy = remote(own_lat, lat.at[here, 2 - d], lat_send.at[index], lat_recv.at[index], device)
-            go(copy, near.get(d))
-            lat_waits.append((near.get(-d), copy))
-            index += 1
-    lat_count = index
+    for index, (d, group) in enumerate(((1, chan), (-1, chan), (1, far_chan), (-1, far_chan), (0, far_chan))):
+        device = (shifted[d] if d else tile, group)
+        copy = remote(own_lat, lat.at[here, 2 - d], lat_send.at[index], lat_recv.at[index], device)
+        go(copy, near.get(d))
+        lat_waits.append((near.get(-d), copy))
     go(remote(win.at[here], win.at[here], par_send.at[0], par_recv.at[0], far))
 
     def exchange_copy(which, src, dst, number, device):
@@ -273,12 +263,23 @@
 
     send_own(0, held_a, held_a_rim)
 
+    between = near[-1] & near[1]
+    for d in (1, -1):
+        for number in ((0, 2) if d == 1 else (1, 3)):
+            guarded(lat_waits[number][0], lat_waits[number][1].wait_recv)
+        copy = remote(
+            lat.at[both, 2 - d], lat.at[both, 2 - 2 * d], lat_send.at[5 + (d < 0)], lat_recv.at[5 + (d < 0)],
+            (shifted[d], chan),
+        )
+        go(copy, between)
+        lat_waits.append((near[-2 * d], copy))
     remote(win.at[here], win.at[there], par_send.at[0], par_recv.at[0], far).wait_recv()
     go(remote(win.at[both], win.at[both], par_send.at[1], par_recv.at[1], mate))
-    for condition, copy in lat_waits:
+    for condition, copy in lat_waits[4:]:
         guarded(condition, copy.wait_recv)
-    go(remote(lat.at[both], lat.at[both], lat_send.at[lat_count], lat_recv.at[lat_count], mate))
+    go(remote(lat.at[both], lat.at[both], lat_send.at[7], lat_recv.at[7], mate))
     pass_on(0, held_a, held_a_rim)
+    pack(1, held_b, 4)
     send_own(1, held_b, held_b_rim)
 
     lane = lax.broadcasted_iota(jnp.int32, (1, LANES), 1)
@@ -303,13 +304,16 @@
     bias_in_column = full_column(0)
     gain_a_column = full_column(1)
     gain_b_column = full_column(2)
+    own_rows = jnp.concatenate([bias_a[...], bias_b[...], jnp.zeros((6, width), F32)], axis=0)
+    par[...] = padded(own_rows, 128)
+    par[2:3] = padded(bias_up[...], 128)
     own_columns = par[...].T
     bias_a_column = own_columns[:width, 0:1]
     bias_b_column = own_columns[:width, 1:2]
     bias_up_column = own_columns[: width // 2, 2:3]
     stem_left = stem_left[:, :depth]
 
-    remote(lat.at[both], lat.at[mates], lat_send.at[lat_count], lat_recv.at[lat_count], mate).wait_recv()
+    remote(lat.at[both], lat.at[mates], lat_send.at[7], lat_recv.at[7], mate).wait_recv()
     depth = GROUPS * own_lat.shape[0]
     place = lax.broadcasted_iota(jnp.int32, (depth, depth), 0)
     taken = lax.broadcasted_iota(jnp.int32, (depth, depth), 1)
@@ -355,8 +359,6 @@
                 stem[frame] = values.reshape(GROUPS, C // GROUPS, LANES)
             maps[2 + frame, step] = activate(values, gain_a_column, step)
 
-    take_mate(0, held_a, held_a_rim)
-
     def windows(own, rim, frame):
         low, high = (jnp.concatenate([rim[number, side] for number in order], axis=0) for side in (LOW, HIGH))
         middle = jnp.concatenate([own[number, frame] for number in order], axis=0)
@@ -384,10 +386,14 @@
         result = result + jnp.where(last_column, 0.0, pltpu.roll(acc[2 * width :], LANES - 2, 1))
         return (result + bias_column).astype(BF16)[:, :span]
 
+    local[0].wait()
+    early[0] = taps(wa, 0, (2,))
+    early[1] = taps(wa, 1, (1, 2))
+    take_mate(0, held_a, held_a_rim)
     load_windows(held_a, held_a_rim)
-    local[0].wait()
     for frame in range(2):
-        swap_a[here, frame] = finish(taps(wa, frame, (0, 1, 2)), frame, bias_a_column, None)
+        acc = early[frame] + taps(wa, frame, (0, 1) if frame == 0 else (0,))
+        swap_a[here, frame] = finish(acc, frame, bias_a_column, None)
     pack(2, swap_a)
     send_own(2, swap_a, swap_a_rim)
 
@@ -514,8 +520,8 @@
             pltpu.VMEM((2, 4 * width // 2, 2 * C), BF16),
             pltpu.VMEM((2 * LANES, 2 * LANES), BF16),
             dma((5,)),
-            dma((10,)),
-            dma((10,)),
+            dma((8,)),
+            dma((8,)),
             dma((2,)),
             dma((2,)),
             dma((4, 9)),

time: 48.4 us -> 46.9 us (0.969)
  the two profiles are of different devices: /device:TPU:97 before, /device:TPU:7 now
where the time goes in v3:
time: 46.9 us; the launch traced here: 46.4 us
  Pallas kernels  44.7 us (95%)
  local copies, waits for them, and re-layouts  1.62 us (3%)
    pallas_call x1, Pallas kernels, shards(): pl.pallas_call(functools.partial(body, tiles, span), out_shape=jax.ShapeD...  44.7 us
    unnamed x1, local copies, waits for them, and re-layouts  1.62 us

profile of v3, /device:TPU:7, one launch (start us, length us, event | category | flops | bytes accessed | tf_op | source)
XLA Modules:
  0.0 46.4 jit_solution(7778285896774219304)
XLA Ops:
  0.0 44.7 %shard_map.136 = bf16[2,48,900]{2,1,0:T(8,128)(2,1)} custom-call(bf16[2,4,225]{2,1,0:T(4,128)(2,1)} %latent.1, bf16[2,4,225]{2,1,0:T(4,128)(2,1)} %latent_cache.1, bf16[27,16,96]{2,1,0:T(8,128)(2,1)} %bitcast.15, f32[1,96]{1,0:T(1,128)} %bitcast.16, bf16[2,96,225]{2,1,0:T(8,128)(2,1)} %cache_a.1, f32[1,96]{1,0:T(1,128)} %bitcast.17, ...), custom_call_target="tpu_custom_call" | custom-call | tf_op jit(solution)/shard_map/pallas_call | solution.py:495
  44.7 1.6 %copy.16 = bf16[2,48,900]{2,1,0:T(8,128)(2,1)} copy(bf16[2,48,900]{2,1,0:T(8,128)(2,1)} %shard_map.136) | data formatting | bytes 345600

commit v4 on v3

--- a/solution.py
+++ b/solution.py
@@ -95,21 +95,30 @@
 def body(
     tiles,
     span,
+    latent_hbm,
+    latent_cache_hbm,
+    weight_in_hbm,
+    bias_in_hbm,
+    cache_a,
+    gain_a_hbm,
+    weight_a,
+    bias_a_hbm,
+    cache_b,
+    gain_b_hbm,
+    weight_b,
+    bias_b_hbm,
+    weight_up,
+    bias_up_hbm,
+    out,
     latent,
     latent_cache,
     weight_in,
     bias_in,
-    cache_a,
     gain_a,
-    weight_a,
     bias_a,
-    cache_b,
     gain_b,
-    weight_b,
     bias_b,
-    weight_up,
     bias_up,
-    out,
     own_lat,
     lat,
     win,
@@ -188,7 +197,20 @@
         pltpu.make_async_copy(cache_a, held_a.at[here], loc_sem.at[3]),
         pltpu.make_async_copy(cache_b, held_b.at[here], loc_sem.at[4]),
     ]
-    for number in (3, 4, 0, 1, 2):
+    fetched = (
+        (latent_hbm, latent),
+        (latent_cache_hbm, latent_cache),
+        (weight_in_hbm, weight_in),
+        (bias_in_hbm, bias_in),
+        (gain_a_hbm, gain_a),
+        (gain_b_hbm, gain_b),
+        (bias_a_hbm, bias_a),
+        (bias_b_hbm, bias_b),
+        (bias_up_hbm, bias_up),
+    )
+    for number, (src, dst) in enumerate(fetched):
+        local.append(pltpu.make_async_copy(src, dst, loc_sem.at[5 + number]))
+    for number in (5, 6, 7, 3, 8, 9, 10, 11, 12, 13, 4, 0, 1, 2):
         local[number].start()
 
     def pack(which, buf, waited=None):
@@ -196,6 +218,8 @@
             local[waited].wait()
         packs[which, 0], packs[which, 1] = rim_packs(buf[here, 0], buf[here, 1], span)
 
+    for copy in local[5:]:
+        copy.wait()
     own_lat[...] = jnp.concatenate(
         [latent_cache[0].astype(F32), latent_cache[1].astype(F32), latent[0].astype(F32), latent[1].astype(F32)],
         axis=0,
@@ -495,9 +519,14 @@
     return pl.pallas_call(
         functools.partial(body, tiles, span),
         out_shape=jax.ShapeDtypeStruct((2, width // 2, 4 * span), BF16),
-        in_specs=[vmem, vmem, vmem, vmem, hbm, vmem, hbm, vmem, hbm, vmem, hbm, vmem, hbm, vmem],
+        in_specs=[hbm] * 14,
         out_specs=vmem,
         scratch_shapes=[
+            pltpu.VMEM(latent.shape, BF16),
+            pltpu.VMEM(latent.shape, BF16),
+            pltpu.VMEM((27, weight_in.shape[4], width), BF16),
+            *[pltpu.VMEM((1, width), F32)] * 5,
+            pltpu.VMEM((1, width // 2), F32),
             pltpu.VMEM((4 * small, span), BF16),
             pltpu.VMEM((GROUPS, 5, 4 * small, span), BF16),
             pltpu.VMEM((GROUPS, width, depth + 16), BF16),
@@ -519,7 +548,7 @@
             pltpu.VMEM((9, width // 2, C), BF16),
             pltpu.VMEM((2, 4 * width // 2, 2 * C), BF16),
             pltpu.VMEM((2 * LANES, 2 * LANES), BF16),
-            dma((5,)),
+            dma((14,)),
             dma((8,)),
             dma((8,)),
             dma((2,)),
@@ -528,9 +557,10 @@
             dma((4, 9)),
         ],
         compiler_params=pltpu.CompilerParams(
-            collective_id=0, has_side_effects=True, vmem_limit_bytes=56 << 20
+            collective_id=0, has_side_effects=True, vmem_limit_bytes=48 << 20
         ),
     )(
+        *(pltpu.with_memory_space_constraint(operand, pltpu.HBM) for operand in (
         latent,
         latent_cache,
         weight_in.swapaxes(3, 4).reshape(27, -1, width),
@@ -545,7 +575,7 @@
         row(bias_b),
         weight_up.reshape(9, width // 2, C),
         row(bias_up),
-    )
+    )))
 
 
 def solution(mesh):

time: 46.9 us -> 44.4 us (0.947)
  Pallas kernels: 44.7 us -> 43.6 us
  local copies, waits for them, and re-layouts: 1.62 us -> 0.68 us
    pallas_call x1, Pallas kernels: 44.7 us -> 43.6 us  [shards(): pl.pallas_call(functools.partial(body, tiles, span), out_shape=jax.ShapeD...]
    unnamed x1, local copies, waits for them, and re-layouts: 1.62 us -> 0.68 us
where the time goes in v4:
time: 44.4 us; the launch traced here: 44.3 us
  Pallas kernels  43.6 us (98%)
  local copies, waits for them, and re-layouts  0.68 us (2%)
    pallas_call x1, Pallas kernels, shards(): pl.pallas_call(functools.partial(body, tiles, span), out_shape=jax.ShapeD...  43.6 us

profile of v4, /device:TPU:7, one launch (start us, length us, event | category | flops | bytes accessed | tf_op | source)
XLA Modules:
  0.0 44.3 jit_solution(12864485100431274499)
XLA Ops:
  0.0 43.6 %shard_map.136 = bf16[2,48,900]{2,1,0:T(8,128)(2,1)S(1)} custom-call(bf16[2,4,225]{2,1,0:T(4,128)(2,1)} %latent_hbm.1, bf16[2,4,225]{2,1,0:T(4,128)(2,1)} %latent_cache_hbm.1, bf16[27,16,96]{2,1,0:T(8,128)(2,1)} %bitcast.15, f32[1,96]{1,0:T(1,128)} %bitcast.16, bf16[2,96,225]{2,1,0:T(8,128)(2,1)} %cache_a.1, f32[1,96]{1,0:T(1,128)} %bitcast.17, ...), custom_call_target="tpu_custom_call" | custom-call | tf_op jit(solution)/shard_map/pallas_call | solution.py:519
  43.6 0.7 %copy.16 = bf16[2,48,900]{2,1,0:T(8,128)(2,1)} copy(bf16[2,48,900]{2,1,0:T(8,128)(2,1)S(1)} %shard_map.136) | data formatting | bytes 345600

commit v5 on v4

--- a/solution.py
+++ b/solution.py
@@ -396,9 +396,9 @@
     def taps(weight, frame, time_taps):
         acc = None
         for a in time_taps:
-            for b in range(3):
-                term = dot(weight[a * 3 + b], maps[frame + a, b])
-                acc = term if acc is None else acc + term
+            rows = jnp.concatenate([weight[a * 3 + b] for b in range(3)], axis=1)
+            term = dot(rows, maps[frame + a].reshape(3 * C, LANES))
+            acc = term if acc is None else acc + term
         return acc
 
     def finish(acc, frame, bias_column, added):

time: 44.4 us -> 44.2 us (level)
  no operation moved by 1% of the time
where the time goes in v5:
time: 44.2 us; the launch traced here: 44.1 us
  Pallas kernels  43.4 us (98%)
  local copies, waits for them, and re-layouts  0.68 us (2%)
    pallas_call x1, Pallas kernels, shards(): pl.pallas_call(functools.partial(body, tiles, span), out_shape=jax.ShapeD...  43.4 us

profile of v5, /device:TPU:7, one launch (start us, length us, event | category | flops | bytes accessed | tf_op | source)
XLA Modules:
  0.0 44.1 jit_solution(757397641565399619)
XLA Ops:
  0.0 43.4 %shard_map.136 = bf16[2,48,900]{2,1,0:T(8,128)(2,1)S(1)} custom-call(bf16[2,4,225]{2,1,0:T(4,128)(2,1)} %latent_hbm.1, bf16[2,4,225]{2,1,0:T(4,128)(2,1)} %latent_cache_hbm.1, bf16[27,16,96]{2,1,0:T(8,128)(2,1)} %bitcast.15, f32[1,96]{1,0:T(1,128)} %bitcast.16, bf16[2,96,225]{2,1,0:T(8,128)(2,1)} %cache_a.1, f32[1,96]{1,0:T(1,128)} %bitcast.17, ...), custom_call_target="tpu_custom_call" | custom-call | tf_op jit(solution)/shard_map/pallas_call | solution.py:519
  43.4 0.7 %copy.16 = bf16[2,48,900]{2,1,0:T(8,128)(2,1)} copy(bf16[2,48,900]{2,1,0:T(8,128)(2,1)S(1)} %shard_map.136) | data formatting | bytes 345600

commit v6 on v5

--- a/solution.py
+++ b/solution.py
@@ -249,6 +249,7 @@
         guarded(condition, copy.start)
         sends.append((condition, copy))
 
+    go(remote(win.at[here], win.at[here], par_send.at[0], par_recv.at[0], far))
     lat[here, 2] = own_lat[...]
     lat_waits = []
     for index, (d, group) in enumerate(((1, chan), (-1, chan), (1, far_chan), (-1, far_chan), (0, far_chan))):
@@ -256,7 +257,6 @@
         copy = remote(own_lat, lat.at[here, 2 - d], lat_send.at[index], lat_recv.at[index], device)
         go(copy, near.get(d))
         lat_waits.append((near.get(-d), copy))
-    go(remote(win.at[here], win.at[here], par_send.at[0], par_recv.at[0], far))
 
     def exchange_copy(which, src, dst, number, device):
         return remote(src, dst, send_sem.at[which, number], recv_sem.at[which, number], device)
@@ -394,12 +394,9 @@
                 maps[frame, step] = jnp.where(inside(step), values, jnp.zeros_like(values))
 
     def taps(weight, frame, time_taps):
-        acc = None
-        for a in time_taps:
-            rows = jnp.concatenate([weight[a * 3 + b] for b in range(3)], axis=1)
-            term = dot(rows, maps[frame + a].reshape(3 * C, LANES))
-            acc = term if acc is None else acc + term
-        return acc
+        first, count = time_taps[0], len(time_taps)
+        rows = jnp.concatenate([weight[first * 3 + step] for step in range(3 * count)], axis=1)
+        return dot(rows, maps[frame + first : frame + first + count].reshape(3 * count * C, LANES))
 
     def finish(acc, frame, bias_column, added):
         middle = acc[width : 2 * width]

time: 44.2 us -> 44.1 us (level)
  no operation moved by 1% of the time
where the time goes in v6:
time: 44.1 us; the launch traced here: 44 us
  Pallas kernels  43.3 us (98%)
  local copies, waits for them, and re-layouts  0.68 us (2%)
    pallas_call x1, Pallas kernels, shards(): pl.pallas_call(functools.partial(body, tiles, span), out_shape=jax.ShapeD...  43.3 us

profile of v6, /device:TPU:7, one launch (start us, length us, event | category | flops | bytes accessed | tf_op | source)
XLA Modules:
  0.0 44.0 jit_solution(5667584217887558037)
XLA Ops:
  0.0 43.3 %shard_map.136 = bf16[2,48,900]{2,1,0:T(8,128)(2,1)S(1)} custom-call(bf16[2,4,225]{2,1,0:T(4,128)(2,1)} %latent_hbm.1, bf16[2,4,225]{2,1,0:T(4,128)(2,1)} %latent_cache_hbm.1, bf16[27,16,96]{2,1,0:T(8,128)(2,1)} %bitcast.15, f32[1,96]{1,0:T(1,128)} %bitcast.16, bf16[2,96,225]{2,1,0:T(8,128)(2,1)} %cache_a.1, f32[1,96]{1,0:T(1,128)} %bitcast.17, ...), custom_call_target="tpu_custom_call" | custom-call | tf_op jit(solution)/shard_map/pallas_call | solution.py:516
  43.3 0.7 %copy.16 = bf16[2,48,900]{2,1,0:T(8,128)(2,1)} copy(bf16[2,48,900]{2,1,0:T(8,128)(2,1)S(1)} %shard_map.136) | data formatting | bytes 345600
